TPU v7x, 32 devices: a whole 2x2x4 slice. The times are simulated.
32 devices in a mesh: pipe: 2 (over x), dom: 8 (over z, y), rep: 2 (over core).
Axes of the slice: x: 2, y: 2, z: 4, core: 2. Of those that a mesh axis runs over, the one named last changes fastest.
Arguments:
- handoff: bfloat16 [2, 2, 4096, 512], P('pipe', 'rep', 'dom'), may hold values from -6 to 6
- initial: bfloat16 [2, 2, 4096, 512], P('pipe', 'rep', 'dom'), may hold values from -6 to 6
- cotangent: bfloat16 [2, 2, 4096, 512], P('pipe', 'rep', 'dom'), may hold values from -6 to 6
- slots: int32 [2, 2, 4096, 16], P('pipe', 'rep', 'dom'), may hold values from 0 to 639
- edge_weight: bfloat16 [2, 2, 4096, 16], P('pipe', 'rep', 'dom'), may hold values from 0.029907227 to 0.119628906
- boundary: int32 [2, 2, 8, 2, 64], P('pipe', 'rep', 'dom'), may hold values from 0 to 511
- weights: bfloat16 [4, 512, 512], P('pipe'), may hold values from -0.25 to 0.25
Outputs:
- section_out: bfloat16 [2, 2, 4096, 512], P('pipe', 'rep', 'dom')
- input_grad: bfloat16 [2, 2, 4096, 512], P('pipe', 'rep', 'dom')
- weight_grad: bfloat16 [4, 512, 512], P('pipe')
All inputs are finite; a program needn't handle non-finite values.
Results may differ from a plain program's by a relative error of at most 0.013.
Values may be sent and summed in bfloat16 or wider, within the bound.
A program may use at most 64 MiB of HBM per device.

v0:
```python
import math
import jax
import jax.numpy as jnp
from jax import lax
from jax.sharding import PartitionSpec as P

ALPHA = 0.1


def passed_along(shard, axis, by):
    peers = lax.axis_size(axis)
    return lax.ppermute(shard, axis, [(i, (i + by) % peers) for i in range(peers)])


def adjacency(slot_rows, weight_rows, width):
    columns = jnp.arange(width, dtype=jnp.int32)
    total = jnp.zeros((slot_rows.shape[0], width), jnp.float32)
    for k in range(slot_rows.shape[1]):
        total = total + jnp.where(
            slot_rows[:, k][:, None] == columns[None, :],
            weight_rows[:, k][:, None].astype(jnp.float32),
            jnp.float32(0.0),
        )
    return total.astype(jnp.bfloat16)


def silu_slope(value):
    sig = jax.nn.sigmoid(value)
    return sig * (1.0 + value * (1.0 - sig))


def extend(rows, bound):
    to_prev = rows[bound[0]]
    to_next = rows[bound[1]]
    from_prev = passed_along(to_next, "dom", 1)
    from_next = passed_along(to_prev, "dom", -1)
    return jnp.concatenate([from_prev, rows, from_next], axis=0)


def retract(dext, bound, rows, width):
    own = dext[width : width + rows]
    back_prev = dext[:width]
    back_next = dext[width + rows :]
    from_next = passed_along(back_prev, "dom", -1)
    from_prev = passed_along(back_next, "dom", 1)
    return own.at[bound[0]].add(from_prev).at[bound[1]].add(from_next)


def local(handoff, initial, cotangent, slots, edge_weight, boundary, weights):
    f32 = jnp.float32
    rows = handoff.shape[2]
    width = boundary.shape[-1]
    layers = weights.shape[0]
    scale = 1.0 / math.sqrt(rows * lax.axis_size("dom") * lax.axis_size("rep"))
    segment = lax.axis_index("pipe")
    betas = [
        jnp.log(0.5 / (segment * layers + layer + 1).astype(f32) + 1.0) for layer in range(layers)
    ]
    state = passed_along(handoff[0, 0], "pipe", 1)
    start = initial[0, 0].astype(f32)
    adj = adjacency(slots[0, 0], edge_weight[0, 0], rows + 2 * width)
    bound = boundary[0, 0, 0]
    saved = []
    for layer in range(layers):
        beta = betas[layer]
        ext = extend(state, bound)
        agg = jnp.dot(adj, ext, preferred_element_type=f32)
        s_act = ((1.0 - ALPHA) * agg + ALPHA * start).astype(jnp.bfloat16)
        mixed = jnp.dot(s_act, weights[layer], preferred_element_type=f32)
        z_val = (1.0 - beta) * s_act.astype(f32) + beta * mixed
        state = jax.nn.silu(z_val).astype(jnp.bfloat16)
        saved.append((s_act, z_val))
    grad = passed_along(cotangent[0, 0], "pipe", -1)
    finished = [None] * layers
    for layer in reversed(range(layers)):
        beta = betas[layer]
        s_act, z_val = saved[layer]
        dz_val = (grad.astype(f32) * silu_slope(z_val)).astype(jnp.bfloat16)
        term = lax.dot_general(s_act, dz_val, (((0,), (0,)), ((), ())), preferred_element_type=f32)
        summed = lax.psum(term, ("dom", "rep"))
        finished[layer] = (beta * scale * summed).astype(jnp.bfloat16)
        back = lax.dot_general(
            dz_val, weights[layer], (((1,), (1,)), ((), ())), preferred_element_type=f32
        )
        ds_val = (1.0 - beta) * dz_val.astype(f32) + beta * back
        dagg = ((1.0 - ALPHA) * ds_val).astype(jnp.bfloat16)
        dext = lax.dot_general(adj, dagg, (((0,), (0,)), ((), ())), preferred_element_type=f32)
        grad = retract(dext, bound, rows, width).astype(jnp.bfloat16)
    weight_grad = jnp.stack(finished)
    return (state[None, None], grad[None, None], weight_grad)


def solution(mesh):
    in_specs = (
        P("pipe", "rep", "dom", None),
        P("pipe", "rep", "dom", None),
        P("pipe", "rep", "dom", None),
        P("pipe", "rep", "dom", None),
        P("pipe", "rep", "dom", None),
        P("pipe", "rep", "dom", None, None),
        P("pipe", None, None),
    )
    out_specs = (
        P("pipe", "rep", "dom", None),
        P("pipe", "rep", "dom", None),
        P("pipe", None, None),
    )
    return jax.shard_map(local, mesh=mesh, in_specs=in_specs, out_specs=out_specs, check_vma=False)
```

profile of v0, /device:TPU:0, one launch (start us, length us, event | category | flops | bytes accessed | tf_op | source)
XLA Modules:
  0.0 187.4 jit_solution(13704241570418847226)
XLA Ops:
  7.2 3.0 %collective-permute-start.5 = (bf16[512,512]{1,0:T(8,128)(2,1)}, bf16[512,512]{1,0:T(8,128)(2,1)}, u32[]{:S(2)}, u32[]{:S(2)}) collective-permute-start(bf16[512,512]{1,0:T(8,128)(2,1)} %bitcast.118), channel_id=1, source_target_pairs={{0,16},{16,0},{1,17},{17,1},{2,18},{18,2},{3,19},{19,3},{4,20},{20... | collective-permute-start | bytes 1572872 | tf_op jit(solution)/shard_map/ppermute | solution.py:12
  10.3 0.8 fusion.44
  11.1 1.0 slice_convert_fusion.15
  12.1 1.1 fusion.52
  13.2 20.4 %collective-permute-done = bf16[512,512]{1,0:T(8,128)(2,1)S(1)} collective-permute-done((bf16[512,512]{1,0:T(8,128)(2,1)}, bf16[512,512]{1,0:T(8,128)(2,1)S(1)}, u32[]{:S(2)}, u32[]{:S(2)}) %collective-permute-start) | collective-permute-done | bytes 524320 | tf_op jit(solution)/shard_map/ppermute | solution.py:12
  33.6 0.7 gather_fusion.1
  34.3 4.9 %collective-permute-start.2 = (bf16[64,512]{1,0:T(8,128)(2,1)S(1)}, bf16[64,512]{1,0:T(8,128)(2,1)S(1)}, u32[]{:S(2)}, u32[]{:S(2)}) collective-permute-start(bf16[64,512]{1,0:T(8,128)(2,1)S(1)} %gather_fusion.1), channel_id=1, source_target_pairs={{0,14},{2,0},{4,2},{6,4},{8,6},{10,8},{12,10},{14,12},{1,15},{3,1}... | collective-permute-start | bytes 196616 | tf_op jit(solution)/shard_map/ppermute | solution.py:12
  39.2 0.7 gather_fusion
  39.9 2.9 %add_convert_fusion = bf16[512,640]{1,0:T(8,128)(2,1)S(1)} fusion(f32[512]{0:T(512)S(1)} %bitcast.86, s32[512]{0:T(512)S(1)} %bitcast.102, f32[512]{0:T(512)S(1)} %bitcast.87, s32[512]{0:T(512)S(1)} %bitcast.103, f32[512]{0:T(512)S(1)} %bitcast.88, s32[512]{0:T(512)S(1)} %bitcast.104, f32[512]{0:T(512)S(1)} %bitcast.89, s32[512]{0:T(512)S(1)} %bitcast.105, ...), kind=kLoop, calls=%fused_computation.20 | loop fusion | flops 15728640 | bytes 720896 | tf_op jit(solution)/shard_map/convert_element_type | solution.py:24
  43.0 3.9 %collective-permute-done.1 = bf16[64,512]{1,0:T(8,128)(2,1)S(1)} collective-permute-done((bf16[64,512]{1,0:T(8,128)(2,1)S(1)}, bf16[64,512]{1,0:T(8,128)(2,1)S(1)}, u32[]{:S(2)}, u32[]{:S(2)}) %collective-permute-start.1) | collective-permute-done | bytes 65568 | tf_op jit(solution)/shard_map/ppermute | solution.py:12
  48.3 0.7 gather_fusion.3
  49.0 0.7 gather_fusion.2
  49.7 1.6 collective-permute-start.4
  51.9 2.1 %collective-permute-done.4 = bf16[64,512]{1,0:T(8,128)(2,1)S(1)} collective-permute-done((bf16[64,512]{1,0:T(8,128)(2,1)S(1)}, bf16[64,512]{1,0:T(8,128)(2,1)S(1)}, u32[]{:S(2)}, u32[]{:S(2)}) %collective-permute-start.4) | collective-permute-done | bytes 65568 | tf_op jit(solution)/shard_map/ppermute | solution.py:12
  54.0 4.2 %collective-permute-done.3 = bf16[64,512]{1,0:T(8,128)(2,1)S(1)} collective-permute-done((bf16[64,512]{1,0:T(8,128)(2,1)S(1)}, bf16[64,512]{1,0:T(8,128)(2,1)S(1)}, u32[]{:S(2)}, u32[]{:S(2)}) %collective-permute-start.3) | collective-permute-done | bytes 65568 | tf_op jit(solution)/shard_map/ppermute | solution.py:12
  58.8 3.1 %multiply_convert_fusion.4 = (bf16[512,512]{1,0:T(8,128)(2,1)}, bf16[1,1,512,512]{3,2,1,0:T(8,128)(2,1)}) fusion(bf16[512,512]{1,0:T(8,128)(2,1)} %collective-permute-done.5, bf16[512,512]{1,0:T(8,128)(2,1)S(1)} %fusion.7, bf16[2,512,512]{2,1,0:T(8,128)(2,1)S(1)} %copy-done.7, f32[]{:T(128)S(6)} %log.6, f32[]{:T(128)S(6)} %sub.14), kind=kOutput, calls=%fused_computation.48 | convolution fusion | flops 272629760 | bytes 3145736 | tf_op jit(solution)/shard_map/dot_general | solution.py:69
  61.9 2.2 %fusion.22 = f32[640,512]{1,0:T(8,128)S(1)} fusion(bf16[512,640]{1,0:T(8,128)(2,1)S(1)} %copy-done.1, bf16[512,512]{1,0:T(8,128)(2,1)} %get-tuple-element.9, f32[]{:T(128)S(6)} %log.6, f32[]{:T(128)S(6)} %sub.14, bf16[2,512,512]{2,1,0:T(8,128)(2,1)} %param.13), kind=kOutput, calls=%fused_computation.64 | convolution fusion | flops 605552640 | bytes 3538952 | tf_op jit(solution)/shard_map/dot_general | solution.py:87
  64.8 4.7 %collective-permute-start.7 = (f32[64,512]{1,0:T(8,128)}, f32[64,512]{1,0:T(8,128)S(1)}, u32[]{:S(2)}, u32[]{:S(2)}) collective-permute-start(f32[64,512]{1,0:T(8,128)} %get-tuple-element.7), channel_id=1, source_target_pairs={{0,14},{2,0},{4,2},{6,4},{8,6},{10,8},{12,10},{14,12},{1,15},{3,1}... | collective-permute-start | bytes 393224 | tf_op jit(solution)/shard_map/ppermute | solution.py:12
  69.6 2.6 %fusion.56 = f32[512,512]{1,0:T(8,128)} fusion(bf16[512,512]{1,0:T(8,128)(2,1)} %copy-done.5, bf16[512,512]{1,0:T(8,128)(2,1)} %get-tuple-element.9), kind=kOutput, calls=%fused_computation.113 | convolution fusion | flops 268435456 | bytes 2097152 | tf_op jit(solution)/shard_map/dot_general | solution.py:79
  72.6 1.7 scatter_fusion
  74.4 1.4 scatter_fusion.1
  76.8 1.4 fusion.55
  78.2 1.1 copy-done.2
  79.3 1.9 %fusion.9 = f32[640,512]{1,0:T(8,128)S(1)} fusion(bf16[512,640]{1,0:T(8,128)(2,1)S(1)} %copy-done.2, bf16[512,512]{1,0:T(8,128)(2,1)S(1)} %multiply_convert_fusion.2, f32[]{:T(128)S(6)} %log.7, f32[]{:T(128)S(6)} %sub.15, bf16[2,512,512]{2,1,0:T(8,128)(2,1)} %param.13), kind=kOutput, calls=%fused_computation.40 | convolution fusion | flops 605552640 | bytes 3538952 | tf_op jit(solution)/shard_map/dot_general | solution.py:87
  81.3 4.7 %collective-permute-start.9 = (f32[64,512]{1,0:T(8,128)S(1)}, f32[64,512]{1,0:T(8,128)S(1)}, u32[]{:S(2)}, u32[]{:S(2)}) collective-permute-start(f32[64,512]{1,0:T(8,128)S(1)} %get-tuple-element.5), channel_id=1, source_target_pairs={{0,14},{2,0},{4,2},{6,4},{8,6},{10,8},{12,10},{14,12},{1,15},{3,1}... | collective-permute-start | bytes 393224 | tf_op jit(solution)/shard_map/ppermute | solution.py:12
  86.1 4.0 %collective-permute-done.8 = f32[64,512]{1,0:T(8,128)S(1)} collective-permute-done((f32[64,512]{1,0:T(8,128)S(1)}, f32[64,512]{1,0:T(8,128)S(1)}, u32[]{:S(2)}, u32[]{:S(2)}) %collective-permute-start.8) | collective-permute-done | bytes 131104 | tf_op jit(solution)/shard_map/ppermute | solution.py:12
  90.1 1.4 scatter_fusion.2
  91.5 1.4 scatter_fusion.3
  92.8 0.9 convert_bitcast_fusion
  93.7 83.9 %all-reduce.3.cloned.1.call-done = (f32[512,512]{1,0:T(8,128)}, f32[512,512]{1,0:T(8,128)}) async-done(((f32[512,512]{1,0:T(8,128)}, f32[512,512]{1,0:T(8,128)}), (f32[512,512]{1,0:T(8,128)}, f32[512,512]{1,0:T(8,128)})) %all-reduce.3.cloned.1.call-update) | async-done | bytes 2097168 | tf_op jit(solution)/shard_map/psum | solution.py:80
  177.6 1.8 fusion.23
  179.5 1.1 pad_maximum_fusion
  (39 shorter events, 4.9 us)
Async XLA Ops:
  7.2 39.7 %copy-start.8 = (bf16[1,1,512,512]{3,2,1,0:T(8,128)(2,1)S(1)}, bf16[1,1,512,512]{3,2,1,0:T(8,128)(2,1)}, u32[]{:S(2)}) copy-start(bf16[1,1,512,512]{3,2,1,0:T(8,128)(2,1)} %param.8) | copy-start | bytes 1572868
  7.2 170.5 %all-reduce.3.cloned.1.call-start = ((), (), s32[]{:S(2)}) async-start(), calls=%async_computation | async-start | bytes 4194304 | tf_op jit(solution)/shard_map/psum | solution.py:80
  7.2 51.6 %collective-permute-start.5 = (bf16[512,512]{1,0:T(8,128)(2,1)}, bf16[512,512]{1,0:T(8,128)(2,1)}, u32[]{:S(2)}, u32[]{:S(2)}) collective-permute-start(bf16[512,512]{1,0:T(8,128)(2,1)} %bitcast.118), channel_id=1, source_target_pairs={{0,16},{16,0},{1,17},{17,1},{2,18},{18,2},{3,19},{19,3},{4,20},{20... | collective-permute-start | bytes 1572872 | tf_op jit(solution)/shard_map/ppermute | solution.py:12
  10.3 23.4 %collective-permute-start = (bf16[512,512]{1,0:T(8,128)(2,1)}, bf16[512,512]{1,0:T(8,128)(2,1)S(1)}, u32[]{:S(2)}, u32[]{:S(2)}) collective-permute-start(bf16[512,512]{1,0:T(8,128)(2,1)} %bitcast.117), channel_id=1, source_target_pairs={{0,16},{16,0},{1,17},{17,1},{2,18},{18,2},{3,19},{19,3},{4,20},{20... | collective-permute-start | bytes 1572872 | tf_op jit(solution)/shard_map/ppermute | solution.py:12
  34.3 8.7 %collective-permute-start.2 = (bf16[64,512]{1,0:T(8,128)(2,1)S(1)}, bf16[64,512]{1,0:T(8,128)(2,1)S(1)}, u32[]{:S(2)}, u32[]{:S(2)}) collective-permute-start(bf16[64,512]{1,0:T(8,128)(2,1)S(1)} %gather_fusion.1), channel_id=1, source_target_pairs={{0,14},{2,0},{4,2},{6,4},{8,6},{10,8},{12,10},{14,12},{1,15},{3,1}... | collective-permute-start | bytes 196616 | tf_op jit(solution)/shard_map/ppermute | solution.py:12
  39.9 7.0 %collective-permute-start.1 = (bf16[64,512]{1,0:T(8,128)(2,1)S(1)}, bf16[64,512]{1,0:T(8,128)(2,1)S(1)}, u32[]{:S(2)}, u32[]{:S(2)}) collective-permute-start(bf16[64,512]{1,0:T(8,128)(2,1)S(1)} %gather_fusion), channel_id=1, source_target_pairs={{0,2},{2,4},{4,6},{6,8},{8,10},{10,12},{12,14},{14,0},{1,3},{3,5},... | collective-permute-start | bytes 196616 | tf_op jit(solution)/shard_map/ppermute | solution.py:12
  42.9 15.3 %copy-start = (bf16[512,640]{1,0:T(8,128)(2,1)}, bf16[512,640]{1,0:T(8,128)(2,1)S(1)}, u32[]{:S(2)}) copy-start(bf16[512,640]{1,0:T(8,128)(2,1)S(1)} %add_convert_fusion) | copy-start | bytes 1966084
  43.0 4.5 %copy-start.6 = (bf16[2,512,512]{2,1,0:T(8,128)(2,1)S(1)}, bf16[2,512,512]{2,1,0:T(8,128)(2,1)}, u32[]{:S(2)}) copy-start(bf16[2,512,512]{2,1,0:T(8,128)(2,1)} %param.13) | copy-start | bytes 3145732
  47.5 0.8 copy-start.3
  49.7 4.3 %collective-permute-start.4 = (bf16[64,512]{1,0:T(8,128)(2,1)S(1)}, bf16[64,512]{1,0:T(8,128)(2,1)S(1)}, u32[]{:S(2)}, u32[]{:S(2)}) collective-permute-start(bf16[64,512]{1,0:T(8,128)(2,1)S(1)} %gather_fusion.3), channel_id=1, source_target_pairs={{0,14},{2,0},{4,2},{6,4},{8,6},{10,8},{12,10},{14,12},{1,15},{3,1}... | collective-permute-start | bytes 196616 | tf_op jit(solution)/shard_map/ppermute | solution.py:12
  51.2 7.0 %collective-permute-start.3 = (bf16[64,512]{1,0:T(8,128)(2,1)S(1)}, bf16[64,512]{1,0:T(8,128)(2,1)S(1)}, u32[]{:S(2)}, u32[]{:S(2)}) collective-permute-start(bf16[64,512]{1,0:T(8,128)(2,1)S(1)} %gather_fusion.2), channel_id=1, source_target_pairs={{0,2},{2,4},{4,6},{6,8},{8,10},{10,12},{12,14},{14,0},{1,3},{3,5},... | collective-permute-start | bytes 196616 | tf_op jit(solution)/shard_map/ppermute | solution.py:12
  51.9 7.0 %copy-start.7 = (bf16[2,512,512]{2,1,0:T(8,128)(2,1)S(1)}, bf16[2,512,512]{2,1,0:T(8,128)(2,1)}, u32[]{:S(2)}) copy-start(bf16[2,512,512]{2,1,0:T(8,128)(2,1)} %param.13) | copy-start | bytes 3145732
  58.8 3.1 %copy-start.5 = (bf16[512,512]{1,0:T(8,128)(2,1)}, bf16[512,512]{1,0:T(8,128)(2,1)S(1)}, u32[]{:S(2)}) copy-start(bf16[512,512]{1,0:T(8,128)(2,1)S(1)} %fusion.7) | copy-start | bytes 1572868
  58.8 3.1 %copy-start.1 = (bf16[512,640]{1,0:T(8,128)(2,1)S(1)}, bf16[512,640]{1,0:T(8,128)(2,1)}, u32[]{:S(2)}) copy-start(bf16[512,640]{1,0:T(8,128)(2,1)} %copy-done) | copy-start | bytes 1966084
  64.8 7.8 %collective-permute-start.6 = (f32[64,512]{1,0:T(8,128)S(1)}, f32[64,512]{1,0:T(8,128)}, u32[]{:S(2)}, u32[]{:S(2)}) collective-permute-start(f32[64,512]{1,0:T(8,128)S(1)} %get-tuple-element.8), channel_id=1, source_target_pairs={{0,2},{2,4},{4,6},{6,8},{8,10},{10,12},{12,14},{14,0},{1,3},{3,5},... | collective-permute-start | bytes 393224 | tf_op jit(solution)/shard_map/ppermute | solution.py:12
  64.8 9.5 %collective-permute-start.7 = (f32[64,512]{1,0:T(8,128)}, f32[64,512]{1,0:T(8,128)S(1)}, u32[]{:S(2)}, u32[]{:S(2)}) collective-permute-start(f32[64,512]{1,0:T(8,128)} %get-tuple-element.7), channel_id=1, source_target_pairs={{0,14},{2,0},{4,2},{6,4},{8,6},{10,8},{12,10},{14,12},{1,15},{3,1}... | collective-permute-start | bytes 393224 | tf_op jit(solution)/shard_map/ppermute | solution.py:12
  75.7 1.0 copy-start.4
  78.2 1.1 copy-start.2
  81.2 8.8 %collective-permute-start.8 = (f32[64,512]{1,0:T(8,128)S(1)}, f32[64,512]{1,0:T(8,128)S(1)}, u32[]{:S(2)}, u32[]{:S(2)}) collective-permute-start(f32[64,512]{1,0:T(8,128)S(1)} %get-tuple-element.6), channel_id=1, source_target_pairs={{0,2},{2,4},{4,6},{6,8},{8,10},{10,12},{12,14},{14,0},{1,3},{3,5},... | collective-permute-start | bytes 393224 | tf_op jit(solution)/shard_map/ppermute | solution.py:12
  81.3 10.2 %collective-permute-start.9 = (f32[64,512]{1,0:T(8,128)S(1)}, f32[64,512]{1,0:T(8,128)S(1)}, u32[]{:S(2)}, u32[]{:S(2)}) collective-permute-start(f32[64,512]{1,0:T(8,128)S(1)} %get-tuple-element.5), channel_id=1, source_target_pairs={{0,14},{2,0},{4,2},{6,4},{8,6},{10,8},{12,10},{14,12},{1,15},{3,1}... | collective-permute-start | bytes 393224 | tf_op jit(solution)/shard_map/ppermute | solution.py:12
Sparse Core Ops, SparseCore 0:
  78.3 99.2 all-reduce.2
where the time goes:
time: 188 us; the launch traced here: 187 us
  waiting for transfers between devices  119 us (63%)
  starting transfers between devices  19.6 us (10%)
  other arithmetic  14.7 us (8%)
  between operations  14.5 us (8%)
  matrix products  13.1 us (7%)
  local copies, waits for them, and re-layouts  6.55 us (3%)
    psum x1, waiting for transfers between devices, local(): summed = lax.psum(term, ('dom', 'rep'))  83.9 us
    ppermute x10, waiting for transfers between devices, passed_along(): lax.ppermute(shard, axis, [(i, (i + by) % peers) for i in range(peers)])  35 us
    ppermute x10, starting transfers between devices, passed_along(): lax.ppermute(shard, axis, [(i, (i + by) % peers) for i in range(peers)])  19.6 us
    scatter-add x4, other arithmetic, retract(): return own.at[bound[0]].add(from_prev).at[bound[1]].add(from_next)  5.85 us
    dot_general x2, matrix products, local(): lax.dot_general(adj, dagg, (((0,), (0,)), ((), ())), preferred_element_ty...  4.17 us
    dot_general x2, matrix products, local(): lax.dot_general(s_act, dz_val, (((0,), (0,)), ((), ())), preferred_elemen...  4.05 us
  transfers between devices with their start and end apart: 11, of which 7 were waited for; matrix products, arithmetic and copies ran while one was open for 11% of the time, Pallas kernels for 0%

commit v1 on v0

--- a/solution.py
+++ b/solution.py
@@ -5,6 +5,12 @@
 from jax.sharding import PartitionSpec as P
 
 ALPHA = 0.1
+
+
+def gather_and_add(shard, axis):
+    parts = lax.all_gather(shard, axis, axis=0, tiled=False)
+    result = parts.sum(axis=0)
+    return result
 
 
 def passed_along(shard, axis, by):
@@ -77,7 +83,7 @@
         s_act, z_val = saved[layer]
         dz_val = (grad.astype(f32) * silu_slope(z_val)).astype(jnp.bfloat16)
         term = lax.dot_general(s_act, dz_val, (((0,), (0,)), ((), ())), preferred_element_type=f32)
-        summed = lax.psum(term, ("dom", "rep"))
+        summed = gather_and_add(term, ("dom", "rep"))
         finished[layer] = (beta * scale * summed).astype(jnp.bfloat16)
         back = lax.dot_general(
             dz_val, weights[layer], (((1,), (1,)), ((), ())), preferred_element_type=f32

time: 188 us -> 333 us (1.77)
  waiting for transfers between devices: 119 us -> 252 us
  other arithmetic: 14.7 us -> 29.1 us
    all_gather x0 -> x2, waiting for transfers between devices: none -> 212 us  [gather_and_add(): parts = lax.all_gather(shard, axis, axis=0, tiled=False)]
    psum x1 -> x0, waiting for transfers between devices: 83.9 us -> none  [local(): summed = lax.psum(term, ('dom', 'rep'))]
    reduce_sum x0 -> x2, other arithmetic: none -> 15.8 us  [gather_and_add(): result = parts.sum(axis=0)]
    ppermute x10, waiting for transfers between devices: 35 us -> 40.3 us  [passed_along(): lax.ppermute(shard, axis, [(i, (i + by) % peers) for i in range(peers)])]
  transfers between devices with their start and end apart: 11 -> 12, of which waited for: 7 -> 9; matrix products, arithmetic and copies ran while one was open for 11% -> 10% of each run, Pallas kernels for 0% -> 0%
where the time goes in v1:
time: 333 us
  waiting for transfers between devices  252 us (76%)
  other arithmetic  29.1 us (9%)
  starting transfers between devices  20.1 us (6%)
  between operations  14.5 us (4%)
  matrix products  11.5 us (3%)
  local copies, waits for them, and re-layouts  5.49 us (2%)
    all_gather x2, waiting for transfers between devices, gather_and_add(): parts = lax.all_gather(shard, axis, axis=0, tiled=False)  212 us
    ppermute x10, waiting for transfers between devices, passed_along(): lax.ppermute(shard, axis, [(i, (i + by) % peers) for i in range(peers)])  40.3 us
    ppermute x10, starting transfers between devices, passed_along(): lax.ppermute(shard, axis, [(i, (i + by) % peers) for i in range(peers)])  20 us
    reduce_sum x2, other arithmetic, gather_and_add(): result = parts.sum(axis=0)  15.8 us
  transfers between devices with their start and end apart: 12, of which 9 were waited for; matrix products, arithmetic and copies ran while one was open for 10% of the time, Pallas kernels for 0%

profile of v1, /device:TPU:0, one launch (start us, length us, event | category | flops | bytes accessed | tf_op | source)
XLA Modules:
  0.0 332.8 jit_solution(1965105019791179191)
XLA Ops:
  7.2 3.0 collective-permute-start.5
  10.3 0.8 fusion.44
  11.1 1.0 slice_convert_fusion.15
  12.1 1.1 fusion.52
  13.2 20.4 %collective-permute-done = bf16[512,512]{1,0:T(8,128)(2,1)S(1)} collective-permute-done((bf16[512,512]{1,0:T(8,128)(2,1)}, bf16[512,512]{1,0:T(8,128)(2,1)S(1)}, u32[]{:S(2)}, u32[]{:S(2)}) %collective-permute-start) | collective-permute-done | bytes 524320 | tf_op jit(solution)/shard_map/ppermute | solution.py:18
  34.3 4.9 %collective-permute-start.2 = (bf16[64,512]{1,0:T(8,128)(2,1)S(1)}, bf16[64,512]{1,0:T(8,128)(2,1)S(1)}, u32[]{:S(2)}, u32[]{:S(2)}) collective-permute-start(bf16[64,512]{1,0:T(8,128)(2,1)S(1)} %gather_fusion.1), channel_id=1, source_target_pairs={{0,14},{2,0},{4,2},{6,4},{8,6},{10,8},{12,10},{14,12},{1,15},{3,1}... | collective-permute-start | bytes 196616 | tf_op jit(solution)/shard_map/ppermute | solution.py:18
  39.9 2.9 add_convert_fusion
  43.0 3.9 %collective-permute-done.1 = bf16[64,512]{1,0:T(8,128)(2,1)S(1)} collective-permute-done((bf16[64,512]{1,0:T(8,128)(2,1)S(1)}, bf16[64,512]{1,0:T(8,128)(2,1)S(1)}, u32[]{:S(2)}, u32[]{:S(2)}) %collective-permute-start.1) | collective-permute-done | bytes 65568 | tf_op jit(solution)/shard_map/ppermute | solution.py:18
  49.0 0.7 gather_fusion.2
  49.7 1.6 collective-permute-start.4
  51.9 2.1 collective-permute-done.4
  54.0 4.2 %collective-permute-done.3 = bf16[64,512]{1,0:T(8,128)(2,1)S(1)} collective-permute-done((bf16[64,512]{1,0:T(8,128)(2,1)S(1)}, bf16[64,512]{1,0:T(8,128)(2,1)S(1)}, u32[]{:S(2)}, u32[]{:S(2)}) %collective-permute-start.3) | collective-permute-done | bytes 65568 | tf_op jit(solution)/shard_map/ppermute | solution.py:18
  58.8 2.7 multiply_convert_fusion.4
  61.5 1.4 fusion.56
  63.0 2.2 fusion.22
  66.0 4.7 %collective-permute-start.7 = (f32[64,512]{1,0:T(8,128)}, f32[64,512]{1,0:T(8,128)S(1)}, u32[]{:S(2)}, u32[]{:S(2)}) collective-permute-start(f32[64,512]{1,0:T(8,128)} %get-tuple-element.5), channel_id=1, source_target_pairs={{0,14},{2,0},{4,2},{6,4},{8,6},{10,8},{12,10},{14,12},{1,15},{3,1}... | collective-permute-start | bytes 393224 | tf_op jit(solution)/shard_map/ppermute | solution.py:18
  70.8 3.1 collective-permute-done.6
  73.8 1.7 scatter_fusion
  75.6 0.8 collective-permute-done.7
  76.4 1.4 scatter_fusion.1
  78.8 1.5 fusion.55
  80.3 1.9 fusion.9
  82.4 5.1 %collective-permute-start.9 = (f32[64,512]{1,0:T(8,128)S(1)}, f32[64,512]{1,0:T(8,128)S(1)}, u32[]{:S(2)}, u32[]{:S(2)}) collective-permute-start(f32[64,512]{1,0:T(8,128)S(1)} %get-tuple-element.3), channel_id=1, source_target_pairs={{0,14},{2,0},{4,2},{6,4},{8,6},{10,8},{12,10},{14,12},{1,15},{3,1}... | collective-permute-start | bytes 393224 | tf_op jit(solution)/shard_map/ppermute | solution.py:18
  87.6 5.7 %collective-permute-done.8 = f32[64,512]{1,0:T(8,128)S(1)} collective-permute-done((f32[64,512]{1,0:T(8,128)S(1)}, f32[64,512]{1,0:T(8,128)S(1)}, u32[]{:S(2)}, u32[]{:S(2)}) %collective-permute-start.8) | collective-permute-done | bytes 131104 | tf_op jit(solution)/shard_map/ppermute | solution.py:18
  93.3 1.4 scatter_fusion.2
  94.7 1.6 scatter_fusion.3
  96.3 0.9 convert_bitcast_fusion
  97.1 93.0 %all-gather.7.cloned.1.call-done = f32[8192,512]{1,0:T(8,128)} async-done(((f32[512,512]{1,0:T(8,128)}), f32[8192,512]{1,0:T(8,128)}) %all-gather.7.cloned.1.call-update) | async-done | bytes 16777232 | tf_op jit(solution)/shard_map/all_gather | solution.py:11
  190.1 7.9 %reduce_sum.19 = f32[512,512]{1,0:T(8,128)S(1)} reduce(f32[16,512,512]{2,1,0:T(8,128)} %bitcast.85, f32[]{:T(128)} %constant.8.clone.1), dimensions={0}, to_apply=%region_5.6 | reduce | flops 3932160 | bytes 17825796 | tf_op jit(solution)/shard_map/reduce_sum | solution.py:12
  198.1 118.7 %all-gather.5.cloned.1.call-done = f32[8192,512]{1,0:T(8,128)} async-done(((f32[512,512]{1,0:T(8,128)}), f32[8192,512]{1,0:T(8,128)}) %all-gather.5.cloned.1.call-update) | async-done | bytes 16777232 | tf_op jit(solution)/shard_map/all_gather | solution.py:11
  316.9 7.9 %reduce_sum.18 = f32[512,512]{1,0:T(8,128)S(1)} reduce(f32[16,512,512]{2,1,0:T(8,128)} %bitcast.86, f32[]{:T(128)} %constant.8.clone.1), dimensions={0}, to_apply=%region_4.5 | reduce | flops 3932160 | bytes 17825796 | tf_op jit(solution)/shard_map/reduce_sum | solution.py:12
  324.9 1.1 pad_maximum_fusion
  (45 shorter events, 7.0 us)
Async XLA Ops:
  7.2 39.7 %copy-start.8 = (bf16[1,1,512,512]{3,2,1,0:T(8,128)(2,1)S(1)}, bf16[1,1,512,512]{3,2,1,0:T(8,128)(2,1)}, u32[]{:S(2)}) copy-start(bf16[1,1,512,512]{3,2,1,0:T(8,128)(2,1)} %param.8) | copy-start | bytes 1572868
  7.2 182.9 %all-gather.7.cloned.1.call-start = ((), (), s32[]{:S(2)}) async-start(), calls=%async_computation.1 | async-start | bytes 17825792 | tf_op jit(solution)/shard_map/all_gather | solution.py:11
  7.2 51.6 %collective-permute-start.5 = (bf16[512,512]{1,0:T(8,128)(2,1)}, bf16[512,512]{1,0:T(8,128)(2,1)}, u32[]{:S(2)}, u32[]{:S(2)}) collective-permute-start(bf16[512,512]{1,0:T(8,128)(2,1)} %bitcast.122), channel_id=1, source_target_pairs={{0,16},{16,0},{1,17},{17,1},{2,18},{18,2},{3,19},{19,3},{4,20},{20... | collective-permute-start | bytes 1572872 | tf_op jit(solution)/shard_map/ppermute | solution.py:18
  10.3 23.4 %collective-permute-start = (bf16[512,512]{1,0:T(8,128)(2,1)}, bf16[512,512]{1,0:T(8,128)(2,1)S(1)}, u32[]{:S(2)}, u32[]{:S(2)}) collective-permute-start(bf16[512,512]{1,0:T(8,128)(2,1)} %bitcast.121), channel_id=1, source_target_pairs={{0,16},{16,0},{1,17},{17,1},{2,18},{18,2},{3,19},{19,3},{4,20},{20... | collective-permute-start | bytes 1572872 | tf_op jit(solution)/shard_map/ppermute | solution.py:18
  34.3 8.7 %collective-permute-start.2 = (bf16[64,512]{1,0:T(8,128)(2,1)S(1)}, bf16[64,512]{1,0:T(8,128)(2,1)S(1)}, u32[]{:S(2)}, u32[]{:S(2)}) collective-permute-start(bf16[64,512]{1,0:T(8,128)(2,1)S(1)} %gather_fusion.1), channel_id=1, source_target_pairs={{0,14},{2,0},{4,2},{6,4},{8,6},{10,8},{12,10},{14,12},{1,15},{3,1}... | collective-permute-start | bytes 196616 | tf_op jit(solution)/shard_map/ppermute | solution.py:18
  39.9 7.0 %collective-permute-start.1 = (bf16[64,512]{1,0:T(8,128)(2,1)S(1)}, bf16[64,512]{1,0:T(8,128)(2,1)S(1)}, u32[]{:S(2)}, u32[]{:S(2)}) collective-permute-start(bf16[64,512]{1,0:T(8,128)(2,1)S(1)} %gather_fusion), channel_id=1, source_target_pairs={{0,2},{2,4},{4,6},{6,8},{8,10},{10,12},{12,14},{14,0},{1,3},{3,5},... | collective-permute-start | bytes 196616 | tf_op jit(solution)/shard_map/ppermute | solution.py:18
  42.9 15.3 %copy-start = (bf16[512,640]{1,0:T(8,128)(2,1)}, bf16[512,640]{1,0:T(8,128)(2,1)S(1)}, u32[]{:S(2)}) copy-start(bf16[512,640]{1,0:T(8,128)(2,1)S(1)} %add_convert_fusion) | copy-start | bytes 1966084
  43.0 4.5 %copy-start.6 = (bf16[2,512,512]{2,1,0:T(8,128)(2,1)S(1)}, bf16[2,512,512]{2,1,0:T(8,128)(2,1)}, u32[]{:S(2)}) copy-start(bf16[2,512,512]{2,1,0:T(8,128)(2,1)} %param.13) | copy-start | bytes 3145732
  47.5 0.8 copy-start.3
  49.7 4.3 %collective-permute-start.4 = (bf16[64,512]{1,0:T(8,128)(2,1)S(1)}, bf16[64,512]{1,0:T(8,128)(2,1)S(1)}, u32[]{:S(2)}, u32[]{:S(2)}) collective-permute-start(bf16[64,512]{1,0:T(8,128)(2,1)S(1)} %gather_fusion.3), channel_id=1, source_target_pairs={{0,14},{2,0},{4,2},{6,4},{8,6},{10,8},{12,10},{14,12},{1,15},{3,1}... | collective-permute-start | bytes 196616 | tf_op jit(solution)/shard_map/ppermute | solution.py:18
  51.3 7.0 %collective-permute-start.3 = (bf16[64,512]{1,0:T(8,128)(2,1)S(1)}, bf16[64,512]{1,0:T(8,128)(2,1)S(1)}, u32[]{:S(2)}, u32[]{:S(2)}) collective-permute-start(bf16[64,512]{1,0:T(8,128)(2,1)S(1)} %gather_fusion.2), channel_id=1, source_target_pairs={{0,2},{2,4},{4,6},{6,8},{8,10},{10,12},{12,14},{14,0},{1,3},{3,5},... | collective-permute-start | bytes 196616 | tf_op jit(solution)/shard_map/ppermute | solution.py:18
  51.9 7.0 %copy-start.7 = (bf16[2,512,512]{2,1,0:T(8,128)(2,1)S(1)}, bf16[2,512,512]{2,1,0:T(8,128)(2,1)}, u32[]{:S(2)}) copy-start(bf16[2,512,512]{2,1,0:T(8,128)(2,1)} %param.13) | copy-start | bytes 3145732
  61.5 1.5 copy-start.5
  61.5 1.5 copy-start.1
  63.0 253.9 %all-gather.5.cloned.1.call-start = ((), (), s32[]{:S(2)}) async-start(), calls=%async_computation | async-start | bytes 17825792 | tf_op jit(solution)/shard_map/all_gather | solution.py:11
  66.0 7.9 %collective-permute-start.6 = (f32[64,512]{1,0:T(8,128)S(1)}, f32[64,512]{1,0:T(8,128)}, u32[]{:S(2)}, u32[]{:S(2)}) collective-permute-start(f32[64,512]{1,0:T(8,128)S(1)} %get-tuple-element.6), channel_id=1, source_target_pairs={{0,2},{2,4},{4,6},{6,8},{8,10},{10,12},{12,14},{14,0},{1,3},{3,5},... | collective-permute-start | bytes 393224 | tf_op jit(solution)/shard_map/ppermute | solution.py:18
  66.0 10.5 %collective-permute-start.7 = (f32[64,512]{1,0:T(8,128)}, f32[64,512]{1,0:T(8,128)S(1)}, u32[]{:S(2)}, u32[]{:S(2)}) collective-permute-start(f32[64,512]{1,0:T(8,128)} %get-tuple-element.5), channel_id=1, source_target_pairs={{0,14},{2,0},{4,2},{6,4},{8,6},{10,8},{12,10},{14,12},{1,15},{3,1}... | collective-permute-start | bytes 393224 | tf_op jit(solution)/shard_map/ppermute | solution.py:18
  77.8 1.0 copy-start.4
  78.8 1.5 copy-start.2
  82.3 11.0 %collective-permute-start.8 = (f32[64,512]{1,0:T(8,128)S(1)}, f32[64,512]{1,0:T(8,128)S(1)}, u32[]{:S(2)}, u32[]{:S(2)}) collective-permute-start(f32[64,512]{1,0:T(8,128)S(1)} %get-tuple-element.4), channel_id=1, source_target_pairs={{0,2},{2,4},{4,6},{6,8},{8,10},{10,12},{12,14},{14,0},{1,3},{3,5},... | collective-permute-start | bytes 393224 | tf_op jit(solution)/shard_map/ppermute | solution.py:18
  82.4 12.3 %collective-permute-start.9 = (f32[64,512]{1,0:T(8,128)S(1)}, f32[64,512]{1,0:T(8,128)S(1)}, u32[]{:S(2)}, u32[]{:S(2)}) collective-permute-start(f32[64,512]{1,0:T(8,128)S(1)} %get-tuple-element.3), channel_id=1, source_target_pairs={{0,14},{2,0},{4,2},{6,4},{8,6},{10,8},{12,10},{14,12},{1,15},{3,1}... | collective-permute-start | bytes 393224 | tf_op jit(solution)/shard_map/ppermute | solution.py:18
Sparse Core Ops, SparseCore 0:
  63.1 126.9 all-gather.6
  192.2 124.5 all-gather.4
